TPU v7x, 512 devices: a whole 4x8x8 slice. The times are simulated.
512 devices in a mesh: energy: 8 (over y_lo, core), atom: 64 (over y_hi, x, z).
Axes of the slice: x: 4, y: 8 (y_hi: 2, y_lo: 4; y = y_hi * 4 + y_lo), z: 8, core: 2. Of those that a mesh axis runs over, the one named last changes fastest.
Arguments:
- green: bfloat16 [8, 64, 2, 512, 512], P('energy', 'atom'), may hold values from -0.25 to 0.25
- t_ref: bfloat16 [8, 64, 2, 32, 32], P('energy'), may hold values from -0.24748737 to 0.24748737
- radial: bfloat16 [8, 32, 1024], P('energy'), may hold values from -1 to 1
- energy_weight: float32 [8], P('energy'), may hold values from 10 to 60
- potential: float32 [64, 25, 1024], P('atom'), may hold values from -6 to 6
- coupling: float32 [25, 32], replicated, may hold values from -1 to 1
- zone: int32 [64, 15], P('atom'), may hold values from 0 to 63, as said below
- order: int32 [64], replicated, may hold values from 0 to 63, as said below
Outputs:
- mixed: float32 [64, 25, 1024], P('atom')
- final_density: float32 [64, 25, 1024], P('atom')
Inputs may be any that keep to these rules, and one draw needn't show every extreme that they name: `zone`: each row lists 16 - 1 distinct atom ids, none of them the atom at that row's position. `order`: A permutation of the atom ids.
All inputs are finite; a program needn't handle non-finite values.
Results may differ from a plain program's by a relative error of at most 0.035.
Values may be sent and summed in bfloat16 or wider, within the bound.
A program may use at most 64 MiB of HBM per device.

v0:
```python
import jax
import jax.numpy as jnp
from jax import lax
from jax.sharding import PartitionSpec as P

NITER = 4


MIXING = 0.5
STEEPNESS = 0.8


def drive_scale(field, basis, coupling):
    squares = basis.astype(jnp.float32) ** 2
    intersection = jnp.einsum("acr,br->acb", field, squares, precision=lax.Precision.HIGHEST)
    drive = jnp.einsum("acb,cb->ab", intersection, coupling, precision=lax.Precision.HIGHEST)
    return 1.0 + STEEPNESS * jnp.tanh(drive)


def scatter(zone_t, greens, channels):
    count = zone_t.shape[0]
    zone_size = zone_t.shape[1]
    order_size = zone_size * channels
    seed_block = jnp.concatenate([zone_t[:, 0, 0], zone_t[:, 0, 1]], -1).astype(jnp.float32)
    start = (
        jnp.zeros((count, zone_size, channels, 2 * channels), jnp.float32).at[:, 0].set(seed_block)
    )
    stacked = greens.reshape(count, 2 * order_size, order_size)
    iterate = start
    for sweep in range(NITER):
        current = iterate.astype(jnp.bfloat16).reshape(count, order_size, 2 * channels)
        product = jnp.einsum("aij,ajk->aik", stacked, current, preferred_element_type=jnp.float32)
        product = product.reshape(count, 2, zone_size, channels, 2 * channels)
        real_part = product[:, 0, :, :, :channels] - product[:, 1, :, :, channels:]
        imag_part = product[:, 0, :, :, channels:] + product[:, 1, :, :, :channels]
        scattered = jnp.concatenate([real_part, imag_part], -1).astype(jnp.bfloat16)
        left = jnp.einsum(
            "azbc,azcd->azbd", zone_t[:, :, 0], scattered, preferred_element_type=jnp.float32
        )
        right = jnp.einsum(
            "azbc,azcd->azbd", zone_t[:, :, 1], scattered, preferred_element_type=jnp.float32
        )
        update = jnp.concatenate(
            [
                left[..., :channels] - right[..., channels:],
                left[..., channels:] + right[..., :channels],
            ],
            -1,
        )
        iterate = start + update
    return iterate[:, 0, :, channels:]


def density(imag_tau, basis, coupling, weight):
    radial_f = basis.astype(jnp.float32)
    mixed_rows = jnp.einsum("aij,jr->air", imag_tau, radial_f, precision=lax.Precision.HIGHEST)
    paired = radial_f[None] * mixed_rows
    return weight * jnp.einsum("ci,air->acr", coupling, paired, precision=lax.Precision.HIGHEST)


def summed(local_terms):
    return lax.psum(local_terms, "energy")


def body(green, t_ref, radial, energy_weight, potential, coupling, zone, order):
    count = potential.shape[0]
    total = order.shape[0]
    channels = coupling.shape[1]
    atom_rank = lax.axis_index("atom")
    index_list = jnp.arange(total, dtype=jnp.int32)
    position_of = jnp.zeros((total,), jnp.int32).at[order].set(index_list)
    own_positions = atom_rank * count + jnp.arange(count, dtype=jnp.int32)
    zone_pos = jnp.concatenate([own_positions[:, None], position_of[zone]], 1)
    base_all = t_ref[0]
    base_own = lax.dynamic_slice_in_dim(base_all, atom_rank * count, count, 0)
    basis = radial[0]
    weight = energy_weight[0]
    greens = green[0]

    def matrices(field):
        scale = drive_scale(field, basis, coupling)
        own_t = (scale[:, None, :, None] * base_own.astype(jnp.float32)).astype(jnp.bfloat16)
        every = lax.all_gather(own_t, "atom", axis=0, tiled=True)
        return every[zone_pos]

    def path_blocks(field):
        return scatter(matrices(field), greens, channels)

    def one_pass(field):
        return density(path_blocks(field), basis, coupling, weight)

    first = one_pass(potential)
    mixed = (1.0 - MIXING) * potential + MIXING * summed(first)
    final = summed(one_pass(mixed))
    return (mixed, final)


def solution(mesh):
    placed = (
        P("energy", "atom", None, None, None),
        P("energy", None, None, None, None),
        P("energy", None, None),
        P("energy"),
        P("atom", None, None),
        P(),
        P("atom", None),
        P(),
    )
    return jax.shard_map(
        body,
        mesh=mesh,
        in_specs=placed,
        out_specs=(P("atom", None, None), P("atom", None, None)),
        check_vma=False,
    )
```

profile of v0, /device:TPU:1, one launch (start us, length us, event | category | flops | bytes accessed | tf_op | source)
XLA Modules:
  0.0 633.6 jit_solution(14289547260079247878)
XLA Ops:
  7.2 0.8 fusion.69
  8.0 0.7 compare_select_fusion.2
  8.7 1.2 fusion.3
  9.9 0.8 scatter_custom_fusion
  10.7 0.7 gather_fusion
  11.6 0.5 copy.92
  12.2 208.1 %all_gather.6 = bf16[64,2,32,32]{3,2,1,0:T(8,128)(2,1)S(1)} all-gather(bf16[1,2,32,32]{3,2,1,0:T(8,128)(2,1)S(1)} %fusion.43), channel_id=1, replica_groups=mesh['energy'=8,'atom'=64] {'atom'}, dimensions={0}, use_global_device_ids=true | all-gather | bytes 266240 | tf_op jit(solution)/shard_map/all_gather | solution.py:83
  220.3 0.6 gather_fusion.1
  221.1 0.4 convolution_bitcast_fusion.23
  221.9 0.2 convolution_bitcast_fusion.21
  222.2 0.2 convolution_bitcast_fusion.22
  222.8 0.4 convolution_bitcast_fusion.20
  224.6 0.4 convolution_bitcast_fusion.17
  226.3 0.4 convolution_bitcast_fusion.14
  228.6 0.6 copy-done.1
  229.2 0.3 convolution_multiply_fusion.3
  229.5 0.5 copy-done.4
  229.9 0.9 fusion.1
  230.9 90.5 %all-reduce.5.cloned.1.call-done = f32[1,25,1024]{2,1,0:T(8,128)} async-done(((f32[1,25,1024]{2,1,0:T(8,128)}), f32[1,25,1024]{2,1,0:T(8,128)}) %all-reduce.5.cloned.1.call-update) | async-done | bytes 102416 | tf_op jit(solution)/shard_map/psum | solution.py:62
  321.4 0.9 fusion.21
  322.3 0.3 fusion.4
  322.7 200.9 %all_gather.7 = bf16[64,2,32,32]{3,2,1,0:T(8,128)(2,1)S(1)} all-gather(bf16[1,2,32,32]{3,2,1,0:T(8,128)(2,1)S(1)} %fusion.44), channel_id=1, replica_groups=mesh['energy'=8,'atom'=64] {'atom'}, dimensions={0}, use_global_device_ids=true | all-gather | bytes 266240 | tf_op jit(solution)/shard_map/all_gather | solution.py:83
  523.6 0.6 gather_fusion.2
  524.3 0.4 convolution_bitcast_fusion.11
  526.1 0.4 convolution_bitcast_fusion.8
  527.8 0.4 convolution_bitcast_fusion.5
  529.6 0.4 convolution_bitcast_fusion.2
  531.2 0.3 convolution_multiply_fusion.2
  531.4 0.9 fusion
  532.3 0.7 copy.77
  533.1 92.0 %all-reduce.7.cloned.1.call-done = f32[1,25,1024]{2,1,0:T(8,128)} async-done(((f32[1,25,1024]{2,1,0:T(8,128)}), f32[1,25,1024]{2,1,0:T(8,128)}) %all-reduce.7.cloned.1.call-update) | async-done | bytes 102416 | tf_op jit(solution)/shard_map/psum | solution.py:62
  625.1 1.7 copy.78
  (79 shorter events, 10.2 us)
Async XLA Ops:
  7.2 213.9 %copy-start = (bf16[1,1,2,512,512]{4,3,2,1,0:T(8,128)(2,1)S(1)}, bf16[1,1,2,512,512]{4,3,2,1,0:T(8,128)(2,1)}, u32[]{:S(2)}) copy-start(bf16[1,1,2,512,512]{4,3,2,1,0:T(8,128)(2,1)} %param.12) | copy-start | bytes 3145732
  7.2 4.2 copy-start.3
  7.2 314.2 %all-reduce.5.cloned.1.call-start = ((), (), s32[]{:S(2)}) async-start(), calls=%async_computation | async-start | bytes 262144 | tf_op jit(solution)/shard_map/psum | solution.py:62
  228.3 0.8 copy-start.1
  229.2 0.7 copy-start.4
  230.8 90.6 %copy-start.2 = (f32[1,25,1024]{2,0,1:T(1,128)S(1)}, f32[1,25,1024]{2,0,1:T(1,128)}, u32[]{:S(2)}) copy-start(f32[1,25,1024]{2,0,1:T(1,128)} %param.16) | copy-start | bytes 307204
  230.8 394.3 %all-reduce.7.cloned.1.call-start = ((), (), s32[]{:S(2)}) async-start(), calls=%async_computation.1 | async-start | bytes 262144 | tf_op jit(solution)/shard_map/psum | solution.py:62
Sparse Core Ops, SparseCore 0:
  230.9 90.3 all-reduce.4
  532.5 92.5 all-reduce.6
where the time goes:
time: 635 us; the launch traced here: 634 us
  blocking collectives  409 us (64%)
  waiting for transfers between devices  183 us (29%)
  between operations  15.2 us (2%)
  matrix products  11 us (2%)
  local copies, waits for them, and re-layouts  8.49 us (1%)
  other arithmetic  7.25 us (1%)
    all_gather x2, blocking collectives, matrices(): every = lax.all_gather(own_t, 'atom', axis=0, tiled=True)  409 us
    psum x2, waiting for transfers between devices, summed(): return lax.psum(local_terms, 'energy')  183 us
  transfers between devices with their start and end apart: 2, of which 2 were waited for; matrix products, arithmetic and copies ran while one was open for 0% of the time, Pallas kernels for 0%

commit v1 on v0

v1 whole, which is shorter than its diff:
```python
import functools

import jax
import jax.numpy as jnp
from jax import lax
from jax.experimental import pallas as pl
from jax.experimental.pallas import tpu as pltpu
from jax.sharding import PartitionSpec as P

MIXING = 0.5
STEEPNESS = 0.8
F32 = jnp.float32
BF16 = jnp.bfloat16
MESH = pl.DeviceIdType.MESH
NT = (((1,), (1,)), ((), ()))
NN = (((1,), (0,)), ((), ()))
TN = (((0,), (0,)), ((), ()))


def dot(left, right, dims=NN):
    return lax.dot_general(left, right, dims, preferred_element_type=F32)


def split(values):
    high = values.astype(BF16)
    return high, (values - high.astype(F32)).astype(BF16)


def scale_of(drive):
    return 1.0 + STEEPNESS * jnp.tanh(drive)


def kernel(
    energies, atoms, members,
    green, t_ref, radial, weight, potential, coupling, zone, order,
    mixed, final,
    g_v, t_v, rad_v, v_v, w_v, high4, low4, drives, scales_a, scales_b, tau1, tau2, mixed_v, final_v,
    local_sem, drive_send, drive_recv, scale_send, scale_recv, tau_send, tau_recv,
    rad_send, rad_recv, fwd_send, fwd_recv,
):
    channels = radial.shape[1]
    size = members * channels
    plane = atoms // 2
    depth = 8
    width = plane // depth
    me_e = lax.axis_index("energy")
    me_a = lax.axis_index("atom")
    half = me_a // plane
    spot = me_a % plane
    here_x, here_z = spot // depth, spot % depth
    weight_value = weight[0]

    own_rows = pl.ds(pl.multiple_of(me_e * channels, channels), channels)
    loads = [
        pltpu.make_async_copy(potential.at[0], v_v, local_sem.at[0]),
        pltpu.make_async_copy(radial.at[0], rad_v.at[own_rows], local_sem.at[1]),
        pltpu.make_async_copy(t_ref.at[0], t_v, local_sem.at[2]),
        pltpu.make_async_copy(green.at[0, 0], g_v, local_sem.at[3]),
    ]
    for load in loads:
        load.start()

    offsets = [(dx, dz) for dx in range(width) for dz in range(depth) if (dx, dz) != (0, 0)]
    offsets.sort(key=lambda d: -(min(d[0], width - d[0]) + min(d[1], depth - d[1])))

    def plane_peer(offset):
        x, z = (here_x + offset[0]) % width, (here_z + offset[1]) % depth
        return (me_e, half * plane + x * depth + z)

    def line_peer(other_half, offset):
        side = (half + 1) % 2 if other_half else half
        return ((me_e + offset) % energies, side * plane + spot)

    line = [(h, o) for h in (1, 0) for o in range(energies) if (h, o) != (0, 0)]
    barrier = pltpu.get_barrier_semaphore()
    for offset in offsets:
        pl.semaphore_signal(barrier, inc=1, device_id=plane_peer(offset), device_id_type=MESH)
    for h, o in line:
        pl.semaphore_signal(barrier, inc=1, device_id=line_peer(h, o), device_id_type=MESH)

    wanted = [zone[0, k] for k in range(members - 1)]

    def look(j, found):
        atom = order[j]
        return tuple(jnp.where(atom == w, j, f) for w, f in zip(wanted, found))

    found = lax.fori_loop(0, atoms, look, tuple(jnp.int32(0) for _ in wanted))
    positions = [me_a] + list(found)
    slots = [2 * (p % plane) + p // plane for p in positions]

    lane_block = lax.broadcasted_iota(jnp.int32, (1, 128), 1) // channels
    copies = 128 // channels

    loads[0].wait()
    loads[1].wait()
    basis = rad_v[own_rows, :].astype(F32)
    high, low = split(basis * basis)
    high4[...] = jnp.concatenate([high] * copies, 0)
    low4[...] = jnp.concatenate([low] * copies, 0)
    coup = coupling[...]
    coup4 = jnp.concatenate([coup] * copies, 1)
    v_high, v_low = split(v_v[...])
    inter = (
        dot(v_high, high4[...], NT) + dot(v_high, low4[...], NT)
        + dot(v_low, high4[...], NT) + dot(v_low, low4[...], NT)
    )
    drives[half] = jnp.sum(inter * coup4, axis=0, keepdims=True)

    pl.semaphore_wait(barrier, len(offsets) + len(line))

    drive_copy = pltpu.make_async_remote_copy(
        src_ref=drives.at[half], dst_ref=drives.at[half],
        send_sem=drive_send, recv_sem=drive_recv,
        device_id=line_peer(1, 0), device_id_type=MESH,
    )
    drive_copy.start()

    def rows_of(energy):
        return rad_v.at[pl.ds(pl.multiple_of(energy * channels, channels), channels)]

    partner = (me_e + 1 - 2 * (me_e % 2), me_a)

    def forward(k):
        source = rows_of((me_e + energies - 2 * k) % energies)
        return pltpu.make_async_remote_copy(
            src_ref=source, dst_ref=source, send_sem=fwd_send.at[k], recv_sem=fwd_recv.at[k],
            device_id=partner, device_id_type=MESH,
        )

    def across(k):
        return pltpu.make_async_remote_copy(
            src_ref=rows_of(me_e), dst_ref=rows_of(me_e), send_sem=rad_send.at[k], recv_sem=rad_recv.at[k],
            device_id=((me_e + 2 * k) % energies, me_a), device_id_type=MESH,
        )

    chips = energies // 2
    for k in range(1, chips):
        across(k).start()
    forward(0).start()

    drive_copy.wait_recv()

    scales = (scales_a, scales_b)

    def share(step, rows):
        for h in range(2):
            scales[step][2 * spot + h] = rows[h]
        block = scales[step].at[pl.ds(2 * spot, 2)]
        for offset in offsets:
            pltpu.make_async_remote_copy(
                src_ref=block, dst_ref=block, send_sem=scale_send.at[step], recv_sem=scale_recv.at[step],
                device_id=plane_peer(offset), device_id_type=MESH,
            ).start()

    def shared(step, sem):
        block = scales[step].at[pl.ds(0, 2 * len(offsets))]
        pltpu.make_async_copy(block, block, sem.at[step]).wait()

    first_drives = [drives[h] for h in range(2)]
    share(0, [scale_of(d) for d in first_drives])

    loads[2].wait()
    loads[3].wait()
    for k in range(members):
        t_k = t_v[positions[k]]
        t_both = jnp.concatenate([t_k[0], t_k[1]], 0)
        rows = slice(k * channels, (k + 1) * channels)
        by_real = dot(t_both, g_v[0, rows, :])
        by_imag = dot(t_both, g_v[1, rows, :])
        w_v[rows, :size] = (by_real[:channels] - by_imag[channels:]).astype(BF16)
        w_v[rows, size:] = (by_imag[:channels] + by_real[channels:]).astype(BF16)

    own_t = t_v[me_a].astype(F32)
    seed = jnp.concatenate([own_t[0].T, own_t[1].T], 0)
    seed = jnp.concatenate([seed, jnp.zeros((2 * channels, 128 - channels), F32)], 1)
    seed_all = jnp.concatenate([seed, jnp.zeros((2 * channels, size - 128), F32)], 1)
    imag4 = jnp.concatenate([own_t[1]] * copies, 1)
    square = jnp.concatenate([coup, jnp.zeros((32 - coup.shape[0], channels), F32)], 0)
    square4 = jnp.concatenate([square] * copies, 1)
    cross4 = lax.dot_general(square, square4, TN, preferred_element_type=F32, precision=lax.Precision.HIGHEST)
    c_high, c_low = split(coup)
    diagonal = lax.broadcasted_iota(jnp.int32, (channels, 128), 0) == lax.broadcasted_iota(jnp.int32, (channels, 128), 1)

    def turned(x):
        return jnp.concatenate([-x[channels:], x[:channels]], 0)

    def scatter(step):
        pieces = []
        for v in range(members // copies):
            piece = scales[step][slots[copies * v]]
            for q in range(1, copies):
                piece = jnp.where(lane_block == q, scales[step][slots[copies * v + q]], piece)
            pieces.append(piece)
        rows = jnp.concatenate(pieces, 1)
        own = jnp.sum(jnp.where(diagonal, pieces[0], 0.0), axis=1, keepdims=True) * weight_value
        x = (pieces[0] * seed).astype(BF16)
        y = dot(x, w_v[:, :128], NT) + dot(turned(x), w_v[:, size:size + 128], NT)
        x = (rows * (seed_all + y)).astype(BF16)
        for _ in range(2):
            y = dot(x, w_v[:, :size], NT) + dot(turned(x), w_v[:, size:], NT)
            x = (rows * (seed_all + y)).astype(BF16)
        y = (
            dot(w_v[:channels, :size], jnp.concatenate([x[channels:]] * copies, 0), NT)
            + dot(w_v[:channels, size:], jnp.concatenate([x[:channels]] * copies, 0), NT)
        )
        return own * (imag4 + y)

    def pack(tau):
        rows = channels // copies
        packed = tau[:rows]
        for q in range(1, copies):
            packed = jnp.where(lane_block == q, tau[q * rows:(q + 1) * rows], packed)
        return packed.astype(BF16)

    def spread(tau, r):
        tau = tau.astype(F32)
        rows = []
        for q in range(copies):
            shift = (channels * (r - q)) % 128
            moved = tau if shift == 0 else pltpu.roll(tau, shift, 1)
            rows.append(jnp.where(lane_block == r, moved, 0.0))
        return jnp.concatenate(rows, 0).astype(BF16)

    def paired(sets):
        groups = energies // copies
        blocks = [
            jnp.concatenate([spread(taus(g * copies + r), r) for taus in sets for r in range(copies)], 0)
            for g in range(groups)
        ]
        parts = [[] for _ in sets]
        chunk = 256
        for n in range(0, rad_v.shape[1], chunk):
            sums = [None for _ in sets]
            for g in range(groups):
                base = rad_v[g * 128:(g + 1) * 128, n:n + chunk]
                product = dot(blocks[g], base)
                base = base.astype(F32)
                for s in range(len(sets)):
                    for r in range(copies):
                        at = s * 128 + r * channels
                        term = base[r * channels:(r + 1) * channels] * product[at:at + channels]
                        sums[s] = term if sums[s] is None else sums[s] + term
            for s in range(len(sets)):
                parts[s].append(sums[s])
        return [jnp.concatenate(p, 1) for p in parts]

    def density(high_pair, low_pair):
        return dot(c_high, high_pair) + dot(c_high, low_pair) + dot(c_low, high_pair)

    shared(0, scale_recv)
    mine = half * energies + me_e
    tau1[mine] = pack(scatter(0))
    for h, o in line:
        pltpu.make_async_remote_copy(
            src_ref=tau1.at[mine], dst_ref=tau1.at[mine], send_sem=tau_send.at[0], recv_sem=tau_recv.at[0],
            device_id=line_peer(h, o), device_id_type=MESH,
        ).start()
    for k in range(1, chips):
        across(k).wait_recv()
        forward(k).start()
    for k in range(chips):
        forward(k).wait_recv()
    everyone = tau1.at[pl.ds(0, len(line))]
    pltpu.make_async_copy(everyone, everyone, tau_recv.at[0]).wait()

    pairs = paired([lambda n: tau1[n], lambda n: tau1[energies + n]])
    highs, lows = zip(*[split(p) for p in pairs])
    stacked = jnp.concatenate(list(highs) + list(lows), 0)
    inter = dot(stacked, high4[...], NT) + dot(stacked, low4[...], NT)
    rows = []
    for h in range(2):
        both = inter[h * channels:(h + 1) * channels] + inter[(h + 2) * channels:(h + 3) * channels]
        change = jnp.sum(both * cross4, axis=0, keepdims=True)
        rows.append(scale_of((1.0 - MIXING) * first_drives[h] + MIXING * change))
    share(1, rows)

    own_high = jnp.where(half == 0, highs[0].astype(F32), highs[1].astype(F32)).astype(BF16)
    own_low = jnp.where(half == 0, lows[0].astype(F32), lows[1].astype(F32)).astype(BF16)
    mixed_v[...] = (1.0 - MIXING) * v_v[...] + MIXING * density(own_high, own_low)
    mixed_copy = pltpu.make_async_copy(mixed_v, mixed.at[0], local_sem.at[0])
    mixed_copy.start()

    shared(1, scale_recv)
    tau2[me_e] = pack(scatter(1))
    for o in range(1, energies):
        pltpu.make_async_remote_copy(
            src_ref=tau2.at[me_e], dst_ref=tau2.at[me_e], send_sem=tau_send.at[1], recv_sem=tau_recv.at[1],
            device_id=line_peer(0, o), device_id_type=MESH,
        ).start()

    drive_copy.wait_send()
    for k in range(1, chips):
        across(k).wait_send()
    for k in range(chips):
        forward(k).wait_send()
    shared(0, scale_send)
    shared(1, scale_send)
    pltpu.make_async_copy(everyone, everyone, tau_send.at[0]).wait()
    mixed_copy.wait()

    others = tau2.at[pl.ds(0, energies - 1)]
    pltpu.make_async_copy(others, others, tau_recv.at[1]).wait()
    last = paired([lambda n: tau2[n]])[0]
    final_v[...] = density(*split(last))
    final_copy = pltpu.make_async_copy(final_v, final.at[0], local_sem.at[1])
    final_copy.start()
    pltpu.make_async_copy(others, others, tau_send.at[1]).wait()
    final_copy.wait()


def solution(mesh):
    energies, atoms = mesh.shape["energy"], mesh.shape["atom"]

    def body(green, t_ref, radial, energy_weight, potential, coupling, zone, order):
        members = zone.shape[1] + 1
        channels = coupling.shape[1]
        _, nchan, radii = potential.shape
        size = members * channels
        anywhere = pl.BlockSpec(memory_space=pl.ANY)
        scalars = pl.BlockSpec(memory_space=pltpu.SMEM)
        vectors = pl.BlockSpec(memory_space=pltpu.VMEM)
        dma = pltpu.SemaphoreType.DMA
        out = jax.ShapeDtypeStruct(potential.shape, F32)
        return pl.pallas_call(
            functools.partial(kernel, energies, atoms, members),
            out_shape=(out, out),
            in_specs=[anywhere, anywhere, anywhere, scalars, anywhere, vectors, scalars, scalars],
            out_specs=(anywhere, anywhere),
            scratch_shapes=[
                pltpu.VMEM(green.shape[2:], BF16),
                pltpu.VMEM(t_ref.shape[1:], BF16),
                pltpu.VMEM((energies * channels, radii), BF16),
                pltpu.VMEM((nchan, radii), F32),
                pltpu.VMEM((size, 2 * size), BF16),
                pltpu.VMEM((128, radii), BF16),
                pltpu.VMEM((128, radii), BF16),
                pltpu.VMEM((2, 1, 128), F32),
                pltpu.VMEM((atoms, 1, 128), F32),
                pltpu.VMEM((atoms, 1, 128), F32),
                pltpu.VMEM((2 * energies, 8, 128), BF16),
                pltpu.VMEM((energies, 8, 128), BF16),
                pltpu.VMEM((nchan, radii), F32),
                pltpu.VMEM((nchan, radii), F32),
                dma((4,)), dma, dma, dma((2,)), dma((2,)), dma((2,)), dma((2,)),
                dma((energies // 2,)), dma((energies // 2,)), dma((energies // 2,)), dma((energies // 2,)),
            ],
            compiler_params=pltpu.CompilerParams(collective_id=0, has_side_effects=True),
        )(green, t_ref, radial, energy_weight, potential, coupling, zone, order)

    placed = (
        P("energy", "atom", None, None, None),
        P("energy", None, None, None, None),
        P("energy", None, None),
        P("energy"),
        P("atom", None, None),
        P(),
        P("atom", None),
        P(),
    )
    return jax.shard_map(
        body,
        mesh=mesh,
        in_specs=placed,
        out_specs=(P("atom", None, None), P("atom", None, None)),
        check_vma=False,
    )
```

time: 635 us -> 54.1 us (0.09)
  blocking collectives: 409 us -> 0 us
  waiting for transfers between devices: 183 us -> 0 us
  Pallas kernels: 0 us -> 45.1 us
  between operations: 15.2 us -> 1.29 us
  matrix products: 11 us -> 0 us
  other arithmetic: 7.25 us -> 0 us
    all_gather x2 -> x0, blocking collectives: 409 us -> none  [matrices(): every = lax.all_gather(own_t, 'atom', axis=0, tiled=True)]
    psum x2 -> x0, waiting for transfers between devices: 183 us -> none  [summed(): return lax.psum(local_terms, 'energy')]
    pallas_call x0 -> x1, Pallas kernels: none -> 45.1 us  [body(): pl.pallas_call(functools.partial(kernel, energies, atoms, members), out_s...]
    dot_general x29 -> x0, matrix products: 9.87 us -> none  [the longest x8 3.53 us: scatter(): jnp.einsum('aij,ajk->aik', stacked, current, preferred_element_type=jnp.f...]
  transfers between devices with their start and end apart: 2 -> 0, of which waited for: 2 -> 0; matrix products, arithmetic and copies ran while one was open for 0% -> 0% of each run, Pallas kernels for 0% -> 0%
where the time goes in v1:
time: 54.1 us; the launch traced here: 53.8 us
  Pallas kernels  45.1 us (83%)
  local copies, waits for them, and re-layouts  7.43 us (14%)
  between operations  1.29 us (2%)
    pallas_call x1, Pallas kernels, body(): pl.pallas_call(functools.partial(kernel, energies, atoms, members), out_s...  45.1 us
    unnamed x4, local copies, waits for them, and re-layouts  4.99 us
    pallas_call x2, local copies, waits for them, and re-layouts, body(): pl.pallas_call(functools.partial(kernel, energies, atoms, members), out_s...  2.43 us

profile of v1, /device:TPU:1, one launch (start us, length us, event | category | flops | bytes accessed | tf_op | source)
XLA Modules:
  0.0 53.8 jit_solution(10837220422561274336)
XLA Ops:
  1.3 1.6 %copy.11.potential = f32[1,25,1024]{2,1,0:T(8,128)} copy(f32[1,25,1024]{2,0,1:T(1,128)} %param.12) | data formatting | bytes 204800 | tf_op args[4]
  2.8 3.4 %copy.10.t_ref = bf16[1,64,2,32,32]{4,3,2,1,0:T(8,128)(2,1)} copy(bf16[1,64,2,32,32]{1,4,3,2,0:T(8,128)(2,1)} %param.9) | data formatting | bytes 524288 | tf_op args[1]
  6.3 45.1 %shard_map.95 = (f32[1,25,1024]{2,1,0:T(8,128)}, f32[1,25,1024]{2,1,0:T(8,128)}) custom-call(bf16[1,1,2,512,512]{4,3,2,1,0:T(8,128)(2,1)} %green.1, bf16[1,64,2,32,32]{4,3,2,1,0:T(8,128)(2,1)} %copy.10.t_ref, bf16[1,32,1024]{2,1,0:T(8,128)(2,1)} %radial.1, f32[1]{0:T(128)S(6)} %copy.14.weight, f32[1,25,1024]{2,1,0:T(8,128)} %copy.11.potential, ...), custom_call_target="tpu_custom_call" | custom-call | tf_op jit(solution)/shard_map/pallas_call | solution.py:324
  51.3 0.0 copy-start
  51.3 1.7 %copy.12 = f32[1,25,1024]{2,0,1:T(1,128)} copy(f32[1,25,1024]{2,1,0:T(8,128)} %get-tuple-element.2) | data formatting | bytes 204800 | tf_op jit(solution)/shard_map/pallas_call | solution.py:324
  53.0 0.0 copy-done
  53.0 0.7 %copy.13 = f32[1,25,1024]{2,0,1:T(1,128)} copy(f32[1,25,1024]{2,1,0:T(8,128)S(1)} %copy-done) | data formatting | bytes 204800 | tf_op jit(solution)/shard_map/pallas_call | solution.py:324
Async XLA Ops:
  51.3 1.7 %copy-start = (f32[1,25,1024]{2,1,0:T(8,128)S(1)}, f32[1,25,1024]{2,1,0:T(8,128)}, u32[]{:S(2)}) copy-start(f32[1,25,1024]{2,1,0:T(8,128)} %get-tuple-element.3) | copy-start | bytes 307204

commit v2 on v1

--- a/solution.py
+++ b/solution.py
@@ -32,9 +32,10 @@
 
 def kernel(
     energies, atoms, members,
-    green, t_ref, radial, weight, potential, coupling, zone, order,
-    mixed, final,
-    g_v, t_v, rad_v, v_v, w_v, high4, low4, drives, scales_a, scales_b, tau1, tau2, mixed_v, final_v,
+    green, t_ref, radial, weight, potential, coupling_in, zone_in, order_in,
+    both_out,
+    g_v, t_v, rad_v, v_v, w_v, high4, low4, drives, scales_a, scales_b, tau1, tau2, own_pair,
+    picked, coupling, zone, order,
     local_sem, drive_send, drive_recv, scale_send, scale_recv, tau_send, tau_recv,
     rad_send, rad_recv, fwd_send, fwd_recv,
 ):
@@ -48,14 +49,16 @@
     half = me_a // plane
     spot = me_a % plane
     here_x, here_z = spot // depth, spot % depth
-    weight_value = weight[0]
 
     own_rows = pl.ds(pl.multiple_of(me_e * channels, channels), channels)
     loads = [
-        pltpu.make_async_copy(potential.at[0], v_v, local_sem.at[0]),
+        pltpu.make_async_copy(potential, v_v.at[pl.ds(0, potential.shape[0])], local_sem.at[0]),
         pltpu.make_async_copy(radial.at[0], rad_v.at[own_rows], local_sem.at[1]),
-        pltpu.make_async_copy(t_ref.at[0], t_v, local_sem.at[2]),
+        pltpu.make_async_copy(coupling_in, coupling, local_sem.at[4]),
+        pltpu.make_async_copy(t_ref, t_v, local_sem.at[2]),
         pltpu.make_async_copy(green.at[0, 0], g_v, local_sem.at[3]),
+        pltpu.make_async_copy(zone_in, zone, local_sem.at[5]),
+        pltpu.make_async_copy(order_in, order, local_sem.at[6]),
     ]
     for load in loads:
         load.start()
@@ -78,28 +81,35 @@
     for h, o in line:
         pl.semaphore_signal(barrier, inc=1, device_id=line_peer(h, o), device_id_type=MESH)
 
-    wanted = [zone[0, k] for k in range(members - 1)]
-
-    def look(j, found):
-        atom = order[j]
-        return tuple(jnp.where(atom == w, j, f) for w, f in zip(wanted, found))
-
-    found = lax.fori_loop(0, atoms, look, tuple(jnp.int32(0) for _ in wanted))
-    positions = [me_a] + list(found)
-    slots = [2 * (p % plane) + p // plane for p in positions]
-
     lane_block = lax.broadcasted_iota(jnp.int32, (1, 128), 1) // channels
     copies = 128 // channels
-
-    loads[0].wait()
-    loads[1].wait()
+    parity = lane_block % 2
+
+    nchan = coupling.shape[0]
+    chunks = radial.shape[2] // 128
+    whole = nchan // 8 * 8
+
+    def unfolded(ref):
+        return jnp.concatenate([ref[pl.ds(j, nchan, stride=chunks), :] for j in range(chunks)], 1)
+
+    def fold(base, value):
+        ref = both_out
+        for j in range(chunks):
+            piece = value[:, j * 128:(j + 1) * 128]
+            ref[pl.ds(base + j, whole, stride=chunks), :] = piece[:whole]
+            for c in range(whole, nchan):
+                at = base + c * chunks + j
+                ref[at:at + 1, :] = piece[c:c + 1]
+
+    for load in loads[:3]:
+        load.wait()
     basis = rad_v[own_rows, :].astype(F32)
     high, low = split(basis * basis)
     high4[...] = jnp.concatenate([high] * copies, 0)
     low4[...] = jnp.concatenate([low] * copies, 0)
     coup = coupling[...]
     coup4 = jnp.concatenate([coup] * copies, 1)
-    v_high, v_low = split(v_v[...])
+    v_high, v_low = split(unfolded(v_v))
     inter = (
         dot(v_high, high4[...], NT) + dot(v_high, low4[...], NT)
         + dot(v_low, high4[...], NT) + dot(v_low, low4[...], NT)
@@ -134,18 +144,13 @@
         )
 
     chips = energies // 2
-    for k in range(1, chips):
-        across(k).start()
-    forward(0).start()
-
     drive_copy.wait_recv()
 
     scales = (scales_a, scales_b)
 
     def share(step, rows):
-        for h in range(2):
-            scales[step][2 * spot + h] = rows[h]
-        block = scales[step].at[pl.ds(2 * spot, 2)]
+        scales[step][spot] = jnp.where(parity == 0, rows[0], rows[1])
+        block = scales[step].at[pl.ds(spot, 1)]
         for offset in offsets:
             pltpu.make_async_remote_copy(
                 src_ref=block, dst_ref=block, send_sem=scale_send.at[step], recv_sem=scale_recv.at[step],
@@ -153,24 +158,48 @@
             ).start()
 
     def shared(step, sem):
-        block = scales[step].at[pl.ds(0, 2 * len(offsets))]
+        block = scales[step].at[pl.ds(0, len(offsets))]
         pltpu.make_async_copy(block, block, sem.at[step]).wait()
 
     first_drives = [drives[h] for h in range(2)]
     share(0, [scale_of(d) for d in first_drives])
-
-    loads[2].wait()
-    loads[3].wait()
+    for k in range(1, chips):
+        across(k).start()
+    forward(0).start()
+
+    for load in loads[3:]:
+        load.wait()
+    wanted = [zone[0, k] for k in range(members - 1)]
+
+    def look(j, found):
+        atom = order[j]
+        return tuple(jnp.where(atom == w, j, f) for w, f in zip(wanted, found))
+
+    found = lax.fori_loop(0, atoms, look, tuple(jnp.int32(0) for _ in wanted))
+    positions = [me_a] + list(found)
+    spots = [p % plane for p in positions]
+    sides = [p // plane for p in positions]
+
+    member = lax.broadcasted_iota(jnp.int32, (members, atoms), 0)
+    wanted_at = jnp.full((members, atoms), me_a, jnp.int32)
+    for k in range(1, members):
+        wanted_at = jnp.where(member == k, positions[k], wanted_at)
+    one_hot = (lax.broadcasted_iota(jnp.int32, (members, atoms), 1) == wanted_at).astype(F32).astype(BF16)
+    planes = 2 * channels
+    for n in range(planes // copies):
+        block = dot(one_hot, t_v[n * 128:(n + 1) * 128, :], NT)
+        for q in range(copies):
+            moved = block if q == 0 else pltpu.roll(block, 128 - channels * q, 1)
+            picked[pl.ds(n * copies + q, members, stride=planes), :] = moved
     for k in range(members):
-        t_k = t_v[positions[k]]
-        t_both = jnp.concatenate([t_k[0], t_k[1]], 0)
+        t_both = picked[k * planes:(k + 1) * planes, :channels].astype(BF16)
         rows = slice(k * channels, (k + 1) * channels)
         by_real = dot(t_both, g_v[0, rows, :])
         by_imag = dot(t_both, g_v[1, rows, :])
         w_v[rows, :size] = (by_real[:channels] - by_imag[channels:]).astype(BF16)
         w_v[rows, size:] = (by_imag[:channels] + by_real[channels:]).astype(BF16)
 
-    own_t = t_v[me_a].astype(F32)
+    own_t = [picked[:channels, :channels], picked[channels:planes, :channels]]
     seed = jnp.concatenate([own_t[0].T, own_t[1].T], 0)
     seed = jnp.concatenate([seed, jnp.zeros((2 * channels, 128 - channels), F32)], 1)
     seed_all = jnp.concatenate([seed, jnp.zeros((2 * channels, size - 128), F32)], 1)
@@ -184,12 +213,18 @@
     def turned(x):
         return jnp.concatenate([-x[channels:], x[:channels]], 0)
 
+    weight_value = weight[0]
+
     def scatter(step):
+        def row_of(k):
+            both = scales[step][spots[k]]
+            return jnp.where(parity == sides[k], both, pltpu.roll(both, channels, 1))
+
         pieces = []
         for v in range(members // copies):
-            piece = scales[step][slots[copies * v]]
+            piece = row_of(copies * v)
             for q in range(1, copies):
-                piece = jnp.where(lane_block == q, scales[step][slots[copies * v + q]], piece)
+                piece = jnp.where(lane_block == q, row_of(copies * v + q), piece)
             pieces.append(piece)
         rows = jnp.concatenate(pieces, 1)
         own = jnp.sum(jnp.where(diagonal, pieces[0], 0.0), axis=1, keepdims=True) * weight_value
@@ -274,11 +309,8 @@
         rows.append(scale_of((1.0 - MIXING) * first_drives[h] + MIXING * change))
     share(1, rows)
 
-    own_high = jnp.where(half == 0, highs[0].astype(F32), highs[1].astype(F32)).astype(BF16)
-    own_low = jnp.where(half == 0, lows[0].astype(F32), lows[1].astype(F32)).astype(BF16)
-    mixed_v[...] = (1.0 - MIXING) * v_v[...] + MIXING * density(own_high, own_low)
-    mixed_copy = pltpu.make_async_copy(mixed_v, mixed.at[0], local_sem.at[0])
-    mixed_copy.start()
+    for n, parts in enumerate((highs, lows)):
+        own_pair[n] = jnp.where(half == 0, parts[0].astype(F32), parts[1].astype(F32)).astype(BF16)
 
     shared(1, scale_recv)
     tau2[me_e] = pack(scatter(1))
@@ -287,6 +319,8 @@
             src_ref=tau2.at[me_e], dst_ref=tau2.at[me_e], send_sem=tau_send.at[1], recv_sem=tau_recv.at[1],
             device_id=line_peer(0, o), device_id_type=MESH,
         ).start()
+
+    fold(0, (1.0 - MIXING) * unfolded(v_v) + MIXING * density(own_pair[0], own_pair[1]))
 
     drive_copy.wait_send()
     for k in range(1, chips):
@@ -296,16 +330,12 @@
     shared(0, scale_send)
     shared(1, scale_send)
     pltpu.make_async_copy(everyone, everyone, tau_send.at[0]).wait()
-    mixed_copy.wait()
 
     others = tau2.at[pl.ds(0, energies - 1)]
     pltpu.make_async_copy(others, others, tau_recv.at[1]).wait()
     last = paired([lambda n: tau2[n]])[0]
-    final_v[...] = density(*split(last))
-    final_copy = pltpu.make_async_copy(final_v, final.at[0], local_sem.at[1])
-    final_copy.start()
+    fold(nchan * chunks, density(*split(last)))
     pltpu.make_async_copy(others, others, tau_send.at[1]).wait()
-    final_copy.wait()
 
 
 def solution(mesh):
@@ -317,35 +347,42 @@
         _, nchan, radii = potential.shape
         size = members * channels
         anywhere = pl.BlockSpec(memory_space=pl.ANY)
+        vectors = pl.BlockSpec(memory_space=pltpu.VMEM)
         scalars = pl.BlockSpec(memory_space=pltpu.SMEM)
-        vectors = pl.BlockSpec(memory_space=pltpu.VMEM)
         dma = pltpu.SemaphoreType.DMA
-        out = jax.ShapeDtypeStruct(potential.shape, F32)
-        return pl.pallas_call(
+        folded = nchan * radii // 128
+        padded = -(-nchan // 8) * 8 * radii // 128
+        out = pltpu.VMEM((2 * folded, 128), F32)
+        atoms_last = t_ref.transpose(0, 2, 3, 4, 1).reshape(2 * channels * channels, atoms)
+        both = pl.pallas_call(
             functools.partial(kernel, energies, atoms, members),
-            out_shape=(out, out),
-            in_specs=[anywhere, anywhere, anywhere, scalars, anywhere, vectors, scalars, scalars],
-            out_specs=(anywhere, anywhere),
+            out_shape=out,
+            in_specs=[anywhere, anywhere, anywhere, scalars, anywhere, anywhere, anywhere, anywhere],
+            out_specs=vectors,
             scratch_shapes=[
                 pltpu.VMEM(green.shape[2:], BF16),
-                pltpu.VMEM(t_ref.shape[1:], BF16),
+                pltpu.VMEM(atoms_last.shape, BF16),
                 pltpu.VMEM((energies * channels, radii), BF16),
-                pltpu.VMEM((nchan, radii), F32),
+                pltpu.VMEM((padded, 128), F32),
                 pltpu.VMEM((size, 2 * size), BF16),
                 pltpu.VMEM((128, radii), BF16),
                 pltpu.VMEM((128, radii), BF16),
                 pltpu.VMEM((2, 1, 128), F32),
-                pltpu.VMEM((atoms, 1, 128), F32),
-                pltpu.VMEM((atoms, 1, 128), F32),
+                pltpu.VMEM((atoms // 2, 1, 128), F32),
+                pltpu.VMEM((atoms // 2, 1, 128), F32),
                 pltpu.VMEM((2 * energies, 8, 128), BF16),
                 pltpu.VMEM((energies, 8, 128), BF16),
-                pltpu.VMEM((nchan, radii), F32),
-                pltpu.VMEM((nchan, radii), F32),
-                dma((4,)), dma, dma, dma((2,)), dma((2,)), dma((2,)), dma((2,)),
+                pltpu.VMEM((2, channels, radii), BF16),
+                pltpu.VMEM((members * 2 * channels, 128), F32),
+                pltpu.VMEM(coupling.shape, F32),
+                pltpu.SMEM(zone.shape, jnp.int32),
+                pltpu.SMEM(order.shape, jnp.int32),
+                dma((7,)), dma, dma, dma((2,)), dma((2,)), dma((2,)), dma((2,)),
                 dma((energies // 2,)), dma((energies // 2,)), dma((energies // 2,)), dma((energies // 2,)),
             ],
             compiler_params=pltpu.CompilerParams(collective_id=0, has_side_effects=True),
-        )(green, t_ref, radial, energy_weight, potential, coupling, zone, order)
+        )(green, atoms_last, radial, energy_weight, potential.reshape(folded, 128), coupling, zone, order)
+        return both[:folded].reshape(potential.shape), both[folded:].reshape(potential.shape)
 
     placed = (
         P("energy", "atom", None, None, None),

time: 54.1 us -> 45.7 us (0.84)
  local copies, waits for them, and re-layouts: 7.43 us -> 0.69 us
  Pallas kernels: 45.1 us -> 43.6 us
    unnamed x4 -> x0, local copies, waits for them, and re-layouts: 4.99 us -> none
    pallas_call x2 -> x0, local copies, waits for them, and re-layouts: 2.43 us -> none  [body(): pl.pallas_call(functools.partial(kernel, energies, atoms, members), out_s...]
    pallas_call x1, Pallas kernels: 45.1 us -> 43.6 us  [body(): pl.pallas_call(functools.partial(kernel, energies, atoms, members), out_s...]
    slice x0 -> x1, local copies, waits for them, and re-layouts: none -> 0.69 us  [body(): both[folded:].reshape(potential.shape)]
where the time goes in v2:
time: 45.7 us; the launch traced here: 45.5 us
  Pallas kernels  43.6 us (95%)
  between operations  1.29 us (3%)
  local copies, waits for them, and re-layouts  0.69 us (2%)
    pallas_call x1, Pallas kernels, body(): pl.pallas_call(functools.partial(kernel, energies, atoms, members), out_s...  43.6 us

profile of v2, /device:TPU:1, one launch (start us, length us, event | category | flops | bytes accessed | tf_op | source)
XLA Modules:
  0.0 45.5 jit_solution(3655109708825060130)
XLA Ops:
  1.3 43.6 %shard_map.95 = f32[400,128]{1,0:T(8,128)S(1)} custom-call(bf16[1,1,2,512,512]{4,3,2,1,0:T(8,128)(2,1)} %green.1, bf16[2048,64]{1,0:T(8,128)(2,1)} %bitcast.6, bf16[1,32,1024]{2,1,0:T(8,128)(2,1)} %radial.1, f32[1]{0:T(128)S(6)} %copy.14.weight, f32[200,128]{1,0:T(8,128)} %bitcast.9, f32[25,32]{1,0:T(8,128)} %coupling_in.1, s32[1,15]{1,0:T(1,128)} %zone_in.1, ...), custom_call_target="tpu_custom_call" | custom-call | tf_op jit(solution)/shard_map/pallas_call | solution.py:357
  44.9 0.7 %fusion = (f32[200,128]{1,0:T(8,128)}, f32[200,128]{1,0:T(8,128)}) fusion(f32[400,128]{1,0:T(8,128)S(1)} %shard_map.95), kind=kLoop, calls=%fused_computation | loop fusion | bytes 409600 | tf_op jit(solution)/shard_map/slice | solution.py:385
